TPU v7x, 32 devices: a whole 2x2x4 slice. The times are simulated.
32 devices in a mesh: dp: 8 (over z, x), head: 4 (over y, core).
Axes of the slice: x: 2, y: 2, z: 4, core: 2. Of those that a mesh axis runs over, the one named last changes fastest.
Arguments:
- inputs: bfloat16 [8, 1024, 1152], P('dp', 'head'), may hold values from -6 to 6
- segments: int32 [8, 1024], P('dp'), may hold values from 0 to 7, never falling along the last dimension, each value on 1 to 512 neighbouring positions
- cotangent: bfloat16 [8, 1024, 1152], P('dp', 'head'), may hold values from -6 to 6
- query_weight: bfloat16 [1152, 1024], replicated, may hold values from -0.1875 to 0.1875
- key_weight: bfloat16 [1152, 256], replicated, may hold values from -0.1875 to 0.1875
- value_weight: bfloat16 [1152, 256], replicated, may hold values from -0.1875 to 0.1875
- out_weight: bfloat16 [1024, 1152], replicated, may hold values from -0.1875 to 0.1875
- gate_weight: bfloat16 [1152, 6912], P(None, 'head'), may hold values from -0.1875 to 0.1875
- up_weight: bfloat16 [1152, 6912], P(None, 'head'), may hold values from -0.1875 to 0.1875
- down_weight: bfloat16 [6912, 1152], P('head'), may hold values from -0.078125 to 0.078125
- input_gain: float32 [1152], replicated, may hold values from 0.1 to 1.9
- query_gain: float32 [256], replicated, may hold values from 0.1 to 1.9
- key_gain: float32 [256], replicated, may hold values from 0.1 to 1.9
- attn_gain: float32 [1152], replicated, may hold values from 0.1 to 1.9
- pre_ff_gain: float32 [1152], replicated, may hold values from 0.1 to 1.9
- post_ff_gain: float32 [1152], replicated, may hold values from 0.1 to 1.9
Outputs:
- layer_output: bfloat16 [8, 1024, 1152], P('dp', 'head')
- input_grad: float32 [8, 1024, 1152], P('dp', 'head')
- query_weight_grad: float32 [1152, 1024], replicated
- key_weight_grad: float32 [1152, 256], replicated
- value_weight_grad: float32 [1152, 256], replicated
- out_weight_grad: float32 [1024, 1152], replicated
- gate_weight_grad: float32 [1152, 6912], P('dp', 'head')
- up_weight_grad: float32 [1152, 6912], P('dp', 'head')
- down_weight_grad: float32 [6912, 1152], P('head', 'dp')
- input_gain_grad: float32 [1152], replicated
- query_gain_grad: float32 [256], replicated
- key_gain_grad: float32 [256], replicated
- attn_gain_grad: float32 [1152], replicated
- pre_ff_gain_grad: float32 [1152], replicated
- post_ff_gain_grad: float32 [1152], replicated
Inputs may be any that keep to these rules, and one draw needn't show every extreme that they name: `segments`: within a row the document numbers never fall; each of the 8 documents has 1 to 512 tokens, and one has exactly 512.
All inputs are finite; a program needn't handle non-finite values.
Results may differ from a plain program's by a relative error of at most 0.02.
Values may be sent and summed in bfloat16 or wider, within the bound.
No kernel may reach another device: no remote copies, remote signals or barrier semaphores. Data moves between devices by JAX's collectives and lax.ppermute only.
A program may use at most 192 MiB of HBM per device.

v0:
```python
from functools import partial
import jax
import jax.numpy as jnp
from jax import lax
from jax.sharding import PartitionSpec as P

EPSILON = 1e-06
ROPE_BASE = 1000000.0
MASKED = -1e30


def for_sending(x):
    return jax.tree.map(lambda a: a.astype(jnp.bfloat16) if a.dtype == jnp.float32 else a, x)


def rms_norm(values, gain):
    return values * lax.rsqrt(jnp.mean(values * values, axis=-1, keepdims=True) + EPSILON) * gain


def positions_of(segment_ids):
    count = segment_ids.shape[0]
    position_index = jnp.arange(count, dtype=jnp.int32)
    previous = jnp.concatenate([segment_ids[:1] - 1, segment_ids[:-1]])
    starts = jnp.where(segment_ids != previous, position_index, 0)
    return position_index - lax.cummax(starts, axis=0)


def rotary(values, positions, sign):
    half_width = values.shape[-1] // 2
    frequency = ROPE_BASE ** (-2.0 * jnp.arange(half_width, dtype=jnp.float32) / values.shape[-1])
    angle = positions.astype(jnp.float32)[:, None] * frequency[None, :]
    cosine_part = jnp.cos(angle)
    sine_part = jnp.sin(angle) * sign
    if values.ndim == 3:
        cosine_part = cosine_part[:, None, :]
        sine_part = sine_part[:, None, :]
    leading = values[..., :half_width]
    trailing = values[..., half_width:]
    return jnp.concatenate(
        [
            leading * cosine_part - trailing * sine_part,
            trailing * cosine_part + leading * sine_part,
        ],
        axis=-1,
    )


def product(left, right):
    return jnp.dot(left, right, preferred_element_type=jnp.float32)


def product_tn(left, right):
    return lax.dot_general(
        left, right, (((0,), (0,)), ((), ())), preferred_element_type=jnp.float32
    )


def product_nt(left, right):
    return lax.dot_general(
        left, right, (((1,), (1,)), ((), ())), preferred_element_type=jnp.float32
    )


def shards(
    inputs,
    segments,
    cotangent,
    query_weight,
    key_weight,
    value_weight,
    out_weight,
    gate_weight,
    up_weight,
    down_weight,
    input_gain,
    query_gain,
    key_gain,
    attn_gain,
    pre_ff_gain,
    post_ff_gain,
):
    low_type = jnp.bfloat16
    tok_rows = inputs.shape[1]
    head_dim = key_weight.shape[1]
    query_heads = query_weight.shape[1] // head_dim
    seq_len = segments.shape[1]
    block_rows = min(512, seq_len)
    score_scale = head_dim ** (-0.5)
    gelu_tanh = partial(jax.nn.gelu, approximate=True)
    x_rows = inputs[0].astype(jnp.float32)
    segment_ids = segments[0]
    all_positions = positions_of(segment_ids)
    own_start = lax.axis_index("head") * tok_rows
    positions = lax.dynamic_slice_in_dim(all_positions, own_start, tok_rows)
    position_index = jnp.arange(seq_len, dtype=jnp.int32)
    normed, input_pull = jax.vjp(rms_norm, x_rows, input_gain)
    normed_low = normed.astype(low_type)
    q_proj = product(normed_low, query_weight).reshape(tok_rows, query_heads, head_dim)
    k_proj = product(normed_low, key_weight)
    v_low = product(normed_low, value_weight).astype(low_type)
    q_normed, query_pull = jax.vjp(rms_norm, q_proj, query_gain)
    k_normed, key_pull = jax.vjp(rms_norm, k_proj, key_gain)
    q_low = rotary(q_normed, positions, 1.0).astype(low_type)
    k_low = rotary(k_normed, positions, 1.0).astype(low_type)
    query_rows = lax.all_to_all(q_low, "head", split_axis=1, concat_axis=0, tiled=True)[:, 0, :]
    row_segments_all = jnp.take(segment_ids, position_index)
    key_rows, value_rows = (
        lax.all_gather(k_low, "head", axis=0, tiled=True),
        lax.all_gather(v_low, "head", axis=0, tiled=True),
    )

    def masked_scores(start_row):
        row_slice = query_rows[start_row : start_row + block_rows]
        raw_scores = product_nt(row_slice, key_rows) * score_scale
        row_ids = position_index[start_row : start_row + block_rows]
        row_segments = row_segments_all[start_row : start_row + block_rows]
        allowed = (row_segments[:, None] == segment_ids[None, :]) & (
            position_index[None, :] <= row_ids[:, None]
        )
        return jnp.where(allowed, raw_scores, MASKED)

    attended_blocks = []
    log_blocks = []
    for start_row in range(0, seq_len, block_rows):
        masked = masked_scores(start_row)
        row_max = jnp.max(masked, axis=1, keepdims=True)
        exponent = jnp.exp(masked - row_max)
        row_total = jnp.sum(exponent, axis=1, keepdims=True)
        probabilities = (exponent / row_total).astype(low_type)
        attended_blocks.append(product(probabilities, value_rows))
        log_blocks.append(row_max + jnp.log(row_total))
    attended_low = jnp.concatenate(attended_blocks, axis=0).astype(low_type)
    log_totals = jnp.concatenate(log_blocks, axis=0)
    mixed_rows = lax.all_to_all(
        attended_low[:, None, :], "head", split_axis=0, concat_axis=1, tiled=True
    )
    mixed_rows = mixed_rows.reshape(tok_rows, query_heads * head_dim)
    projected = product(mixed_rows, out_weight)
    attn_branch, attn_pull = jax.vjp(rms_norm, projected, attn_gain)
    after_attn = x_rows + attn_branch
    pre_normed, pre_pull = jax.vjp(rms_norm, after_attn, pre_ff_gain)
    rows_all = lax.all_gather(pre_normed.astype(low_type), "head", axis=0, tiled=True)
    gate_act = product(rows_all, gate_weight)
    up_act = product(rows_all, up_weight)
    gelu_gate, gelu_pull = jax.vjp(gelu_tanh, gate_act)
    hidden_low = (gelu_gate * up_act).astype(low_type)
    ff_out = lax.psum_scatter(
        product(
            lax.slice_in_dim(hidden_low, 0, tok_rows * lax.axis_size("head"), axis=0), down_weight
        ).astype(jnp.bfloat16),
        "head",
        scatter_dimension=0,
        tiled=True,
    ).astype(jnp.float32)
    post_branch, post_pull = jax.vjp(rms_norm, ff_out, post_ff_gain)
    layer_out = after_attn + post_branch
    out_grad = cotangent[0].astype(jnp.float32)
    ff_grad, post_gain_grad = post_pull(out_grad)
    ff_grad_all = lax.all_gather(for_sending(ff_grad.astype(low_type)), "head", axis=0, tiled=True)
    down_grad = product_tn(hidden_low, ff_grad_all)
    hidden_grad = product_nt(ff_grad_all, down_weight)
    up_grad_low = (hidden_grad * gelu_gate).astype(low_type)
    gate_grad_low = gelu_pull(hidden_grad * up_act)[0].astype(low_type)
    gate_grad = product_tn(rows_all, gate_grad_low)
    up_grad = product_tn(rows_all, up_grad_low)
    up_slice = lax.slice_in_dim(up_grad_low, 0, tok_rows * lax.axis_size("head"), axis=0)
    pre_grad = lax.psum_scatter(
        (product_nt(gate_grad_low, gate_weight) + product_nt(up_slice, up_weight)).astype(
            jnp.bfloat16
        ),
        "head",
        scatter_dimension=0,
        tiled=True,
    ).astype(jnp.float32)
    after_from_ff, pre_gain_grad = pre_pull(pre_grad)
    after_grad = out_grad + after_from_ff
    projected_grad, attn_gain_grad = attn_pull(after_grad)
    projected_low = projected_grad.astype(low_type)
    out_weight_grad = product_tn(mixed_rows, projected_low)
    mixed_grad = product_nt(projected_low, out_weight).astype(low_type)
    mixed_grad = mixed_grad.reshape(tok_rows, query_heads, head_dim)
    attended_grad = lax.all_to_all(mixed_grad, "head", split_axis=1, concat_axis=0, tiled=True)[
        :, 0, :
    ]
    query_blocks = []
    key_grad = jnp.zeros((seq_len, head_dim), jnp.float32)
    value_grad = jnp.zeros((seq_len, head_dim), jnp.float32)
    for start_row in range(0, seq_len, block_rows):
        masked = masked_scores(start_row)
        probabilities = jnp.exp(masked - log_totals[start_row : start_row + block_rows])
        grad_rows = attended_grad[start_row : start_row + block_rows]
        value_grad = value_grad + product_tn(probabilities.astype(low_type), grad_rows)
        prob_grad = product_nt(grad_rows, value_rows)
        row_delta = jnp.sum(prob_grad * probabilities, axis=1, keepdims=True)
        score_grad = (probabilities * (prob_grad - row_delta)).astype(low_type)
        query_blocks.append(product(score_grad, key_rows) * score_scale)
        key_grad = (
            key_grad
            + product_tn(score_grad, query_rows[start_row : start_row + block_rows]) * score_scale
        )
    query_grad_low = jnp.concatenate(query_blocks, axis=0).astype(low_type)
    query_back = lax.all_to_all(
        query_grad_low[:, None, :], "head", split_axis=0, concat_axis=1, tiled=True
    )
    key_share, value_share = (
        lax.psum_scatter(
            key_grad.astype(jnp.bfloat16), "head", scatter_dimension=0, tiled=True
        ).astype(jnp.float32),
        lax.psum_scatter(
            value_grad.astype(jnp.bfloat16), "head", scatter_dimension=0, tiled=True
        ).astype(jnp.float32),
    )
    q_proj_grad, query_gain_grad = query_pull(
        rotary(query_back.astype(jnp.float32), positions, -1.0)
    )
    key_back = key_share.astype(low_type).astype(jnp.float32)
    k_proj_grad, key_gain_grad = key_pull(rotary(key_back, positions, -1.0))
    q_grad_low = q_proj_grad.reshape(tok_rows, query_heads * head_dim).astype(low_type)
    k_grad_low = k_proj_grad.astype(low_type)
    v_grad_low = value_share.astype(low_type)
    query_weight_grad = product_tn(normed_low, q_grad_low)
    key_weight_grad = product_tn(normed_low, k_grad_low)
    value_weight_grad = product_tn(normed_low, v_grad_low)
    normed_grad = (
        product_nt(q_grad_low, query_weight)
        + product_nt(k_grad_low, key_weight)
        + product_nt(v_grad_low, value_weight)
    )
    input_from_norm, input_gain_grad = input_pull(normed_grad)
    input_grad = after_grad + input_from_norm
    summed = lax.psum(
        (
            query_weight_grad,
            key_weight_grad,
            value_weight_grad,
            out_weight_grad,
            input_gain_grad,
            query_gain_grad,
            key_gain_grad,
            attn_gain_grad,
            pre_gain_grad,
            post_gain_grad,
        ),
        ("dp", "head"),
    )
    gate_share, up_share, down_share = (
        lax.psum_scatter(
            gate_grad.astype(jnp.bfloat16), "dp", scatter_dimension=0, tiled=True
        ).astype(jnp.float32),
        lax.psum_scatter(
            up_grad.astype(jnp.bfloat16), "dp", scatter_dimension=0, tiled=True
        ).astype(jnp.float32),
        lax.psum_scatter(
            down_grad.astype(jnp.bfloat16), "dp", scatter_dimension=1, tiled=True
        ).astype(jnp.float32),
    )
    return (
        layer_out.astype(low_type)[None],
        input_grad[None],
        summed[0],
        summed[1],
        summed[2],
        summed[3],
        gate_share,
        up_share,
        down_share,
        summed[4],
        summed[5],
        summed[6],
        summed[7],
        summed[8],
        summed[9],
    )


def solution(mesh):
    in_specs = (
        P("dp", "head", None),
        P("dp", None),
        P("dp", "head", None),
        P(),
        P(),
        P(),
        P(),
        P(None, "head"),
        P(None, "head"),
        P("head", None),
        P(),
        P(),
        P(),
        P(),
        P(),
        P(),
    )
    out_specs = (
        P("dp", "head", None),
        P("dp", "head", None),
        P(),
        P(),
        P(),
        P(),
        P("dp", "head"),
        P("dp", "head"),
        P("head", "dp"),
        P(),
        P(),
        P(),
        P(),
        P(),
        P(),
    )
    return jax.shard_map(shards, mesh=mesh, in_specs=in_specs, out_specs=out_specs, check_vma=False)
```

profile of v0, /device:TPU:0, one launch (start us, length us, event | category | flops | bytes accessed | tf_op | source)
XLA Modules:
  0.0 871.8 jit_solution(2436494161311775190)
XLA Ops:
  13.7 4.4 copy.65
  18.1 3.6 multiply_reduce_fusion.8
  25.6 4.3 all-to-all-start
  30.5 9.1 %gather_fusion = s32[1024]{0:T(1024)} fusion(s32[1024]{0:T(1024)S(1)} %bitcast.161, s32[1024]{0:T(1024)} %iota_clamp_fusion), kind=kCustom, calls=%fused_computation | custom fusion | bytes 12288 | tf_op jit(solution)/shard_map/jit(_take)/gather | solution.py:106
  43.4 9.0 %all_gather.12 = bf16[1024,256]{0,1:T(8,128)(2,1)} all-gather(bf16[256,256]{0,1:T(8,128)(2,1)S(1)} %pad_maximum_fusion.5), channel_id=1, replica_groups=mesh['dp'=8,'head'=4] {'head'}, dimensions={0}, use_global_device_ids=true | all-gather | bytes 655360 | tf_op jit(solution)/shard_map/all_gather | solution.py:108
  52.5 7.3 all_gather.13
  59.8 2.0 fusion.94
  61.8 1.8 copy.53
  63.6 1.8 copy.54
  65.4 1.9 fusion.96
  73.3 2.0 reshape.403
  75.3 12.3 %all_to_all.54 = bf16[4,2,32768]{2,1,0:T(2,128)(2,1)S(1)} all-to-all(bf16[4,2,32768]{2,1,0:T(2,128)(2,1)} %reshape.403), channel_id=1, replica_groups=mesh['dp'=8,'head'=4] {'head'}, dimensions={0} | all-to-all | bytes 1048576 | tf_op jit(solution)/shard_map/all_to_all | solution.py:134
  89.3 2.1 copy.66
  97.3 24.7 %all-gather.3.cloned.1.call-done = bf16[1024,1152]{1,0:T(8,128)(2,1)} async-done(((bf16[256,1152]{1,0:T(8,128)(2,1)}), bf16[1024,1152]{1,0:T(8,128)(2,1)}) %all-gather.3.cloned.1.call-update) | async-done | bytes 2359312 | tf_op jit(solution)/shard_map/all_gather | solution.py:142
  122.0 7.4 fusion.98
  129.5 7.9 multiply_convert_fusion.1
  139.1 6.3 convolution_convert_fusion.3
  145.5 32.9 %reduce-scatter.8.cloned.1.call-done = bf16[256,1152]{1,0:T(8,128)(2,1)} async-done(((bf16[1024,1152]{1,0:T(8,128)(2,1)}), bf16[256,1152]{1,0:T(8,128)(2,1)}) %reduce-scatter.8.cloned.1.call-update) | async-done | bytes 589840 | tf_op jit(solution)/shard_map/reduce_scatter | solution.py:147
  179.8 2.4 fusion.43
  182.2 2.2 fusion.39
  184.7 23.9 %all-gather.5.cloned.1.call-done = bf16[1024,1152]{1,0:T(8,128)(2,1)} async-done(((bf16[256,1152]{1,0:T(8,128)(2,1)}), bf16[1024,1152]{1,0:T(8,128)(2,1)}) %all-gather.5.cloned.1.call-update) | async-done | bytes 2359312 | tf_op jit(solution)/shard_map/all_gather | solution.py:159
  208.6 14.8 %multiply_convert_fusion = (bf16[1024,1728]{0,1:T(8,128)(2,1)S(1)}, bf16[1024,1728]{0,1:T(8,128)(2,1)S(1)}) fusion(f32[1024,1728]{0,1:T(8,128)} %copy-done.94, f32[1024,1728]{0,1:T(8,128)} %get-tuple-element.71, bf16[1024,1152]{1,0:T(8,128)(2,1)} %all-gather.5.cloned.1.call-done, bf16[1728,1152]{1,0:T(8,128)(2,1)} %param.25), kind=kOutput, calls=%fused_computation.13 | convolution fusion | flops 4119330816 | bytes 27574272 | tf_op jit(solution)/shard_map/dot_general | solution.py:59
  223.5 5.2 fusion.99
  228.7 6.8 add_convert_fusion
  235.6 33.0 %reduce-scatter.10.cloned.1.call-done = bf16[256,1152]{1,0:T(8,128)(2,1)} async-done(((bf16[1024,1152]{1,0:T(8,128)(2,1)}), bf16[256,1152]{1,0:T(8,128)(2,1)}) %reduce-scatter.10.cloned.1.call-update) | async-done | bytes 589840 | tf_op jit(solution)/shard_map/reduce_scatter | solution.py:167
  268.5 2.5 fusion.34
  271.8 3.9 multiply_reduce_fusion.2
  277.8 4.3 all-to-all-start.2
  282.2 8.8 %all-to-all-done.2 = bf16[256,4,256]{2,0,1:T(8,128)(2,1)} async-done(((bf16[256,4,256]{2,0,1:T(8,128)(2,1)}), bf16[256,4,256]{2,0,1:T(8,128)(2,1)}, u32[]{:S(2)}, u32[]{:S(2)}) %all-to-all-start.2) | async-done | bytes 524320 | tf_op jit(solution)/shard_map/all_to_all | solution.py:182
  299.1 2.2 fusion.52
  302.8 9.4 %convolution_convert_fusion = bf16[1728,1152]{0,1:T(8,128)(2,1)} fusion(bf16[1024,1728]{0,1:T(8,128)(2,1)} %copy-done.93, bf16[1024,1152]{1,0:T(8,128)(2,1)} %all-gather.5.cloned.1.call-done), kind=kOutput, calls=%fused_computation.3 | convolution fusion | flops 4078854144 | bytes 9879552 | tf_op jit(solution)/shard_map/dot_general | solution.py:53
  313.9 8.4 convolution_convert_fusion.1
  322.4 8.2 convolution_convert_fusion.2
  334.9 3.5 all-to-all-start.3
  338.4 3.0 fusion.102
  341.5 8.0 all-to-all-done.3
  357.1 2.4 fusion.85
  359.5 3.1 fusion.59
  367.3 42.1 %all-reduce = (f32[1152]{0:T(1024)}, f32[256]{0:T(256)}, f32[256]{0:T(256)}, f32[1152]{0:T(1024)}, f32[1152]{0:T(1024)}, /*index=5*/f32[1152]{0:T(1024)}) all-reduce(f32[1152]{0:T(1024)S(1)} %get-tuple-element.21, f32[256]{0:T(256)S(1)} %get-tuple-element.17, ...), channel_id=1, replica_groups=mesh['dp'=8,'head'=4] {'dp','head'}, use_global_device_ids=true, to_apply=%region_32.33 | all-reduce | flops 5120 | bytes 40960 | tf_op jit(solution)/shard_map/psum | solution.py:231
  410.7 29.7 %reduce-scatter.20.cloned.1.call-done = bf16[1728,144]{0,1:T(8,128)(2,1)} async-done(((bf16[1728,1152]{0,1:T(8,128)(2,1)}), bf16[1728,144]{0,1:T(8,128)(2,1)}) %reduce-scatter.20.cloned.1.call-update) | async-done | bytes 497680 | tf_op jit(solution)/shard_map/reduce_scatter | solution.py:253
  440.5 2.1 convert_element_type.202
  442.5 89.1 %reduce-scatter.18.cloned.1.call-done = bf16[144,1728]{1,0:T(8,128)(2,1)} async-done(((bf16[1152,1728]{1,0:T(8,128)(2,1)}), bf16[144,1728]{1,0:T(8,128)(2,1)}) %reduce-scatter.18.cloned.1.call-update) | async-done | bytes 497680 | tf_op jit(solution)/shard_map/reduce_scatter | solution.py:250
  531.6 2.1 convert_element_type.200
  533.7 89.1 %reduce-scatter.16.cloned.1.call-done = bf16[144,1728]{1,0:T(8,128)(2,1)} async-done(((bf16[1152,1728]{1,0:T(8,128)(2,1)}), bf16[144,1728]{1,0:T(8,128)(2,1)}) %reduce-scatter.16.cloned.1.call-update) | async-done | bytes 497680 | tf_op jit(solution)/shard_map/reduce_scatter | solution.py:247
  622.7 2.1 convert_element_type.198
  624.8 228.5 %all-reduce.4.cloned.1.call-done = (f32[1152,1024]{1,0:T(8,128)}, f32[1152,256]{1,0:T(8,128)}, f32[1152,256]{1,0:T(8,128)}, f32[1024,1152]{1,0:T(8,128)}) async-done(((f32[1152,1024]{1,0:T(8,128)}, f32[1152,256]{1,0:T(8,128)}, f32[1152,256]{1,0:T(8,128)}, f32[1024,1152]{1,0:T(8,128)}), (f32[1152,1024]{1,0:T(8,128)}, f32[1152,256]{1,0:T(8,128)}, f32[1152,256]{1,0:T(8,128)}, ...) | async-done | bytes 11796496 | tf_op jit(solution)/shard_map/psum | solution.py:231
  853.3 5.4 copy.76
  861.4 2.4 copy.79
  (306 shorter events, 66.6 us)
Async XLA Ops:
  7.2 85.5 %copy-start = (bf16[1024,1152]{1,0:T(8,128)(2,1)S(1)}, bf16[1024,1152]{1,0:T(8,128)(2,1)}, u32[]{:S(2)}) copy-start(bf16[1024,1152]{1,0:T(8,128)(2,1)} %param.22) | copy-start | bytes 7077892
  7.2 14.8 %copy-start.84 = (f32[128]{0:T(128)}, f32[128]{0:T(128)S(1)}, u32[]{:S(2)}) copy-start(f32[128]{0:T(128)S(1)} %multiply_power_fusion) | copy-start | bytes 1540
  9.8 8.3 copy-start.50
  13.7 4.4 copy-start.80
  13.7 8.2 copy-start.27
  13.7 8.1 copy-start.55
  13.7 4.4 copy-start.3
  18.1 5.1 copy-start.61
  24.6 5.9 copy-start.2
  25.6 34.1 %all-to-all-start = ((bf16[256,4,256]{0,2,1:T(8,128)(2,1)}), bf16[256,4,256]{0,2,1:T(8,128)(2,1)}, u32[]{:S(2)}, u32[]{:S(2)}) async-start(bf16[256,4,256]{0,2,1:T(8,128)(2,1)} %pad_maximum_fusion.1), calls=%async_computation | async-start | bytes 1048576 | tf_op jit(solution)/shard_map/all_to_all | solution.py:105
  29.9 92.1 %all-gather.3.cloned.1.call-start = ((), (), s32[]{:S(2)}) async-start(), calls=%async_computation.11 | async-start | bytes 2949120 | tf_op jit(solution)/shard_map/all_gather | solution.py:142
  30.5 10.9 %copy-start.40 = (bf16[1152,256]{1,0:T(8,128)(2,1)S(1)}, bf16[1152,256]{1,0:T(8,128)(2,1)}, u32[]{:S(2)}) copy-start(bf16[1152,256]{1,0:T(8,128)(2,1)} %param.21) | copy-start | bytes 1769476
  42.5 22.8 %copy-start.83 = (s32[512]{0:T(512)S(1)}, s32[512]{0:T(512)}, u32[]{:S(2)}) copy-start(s32[512]{0:T(512)} %slice.99) | copy-start | bytes 6148
  59.7 10.6 %copy-start.19 = (bf16[1024,256]{1,0:T(8,128)(2,1)}, bf16[1024,256]{1,0:T(8,128)(2,1)S(1)}, u32[]{:S(2)}) copy-start(bf16[1024,256]{1,0:T(8,128)(2,1)S(1)} %all_gather.13) | copy-start | bytes 1572868
  95.1 34.3 %copy-start.63 = (f32[256]{0:T(256)}, f32[256]{0:T(256)S(1)}, u32[]{:S(2)}) copy-start(f32[256]{0:T(256)S(1)} %get-tuple-element.38) | copy-start | bytes 3076
  95.1 34.3 %copy-start.59 = (f32[256]{0:T(256)}, f32[256]{0:T(256)S(1)}, u32[]{:S(2)}) copy-start(f32[256]{0:T(256)S(1)} %fusion.83) | copy-start | bytes 3076
  97.1 81.3 %reduce-scatter.8.cloned.1.call-start = ((), (), s32[]{:S(2)}) async-start(), calls=%async_computation.12 | async-start | bytes 2949120 | tf_op jit(solution)/shard_map/reduce_scatter | solution.py:147
  122.0 7.4 copy-start.88
  122.0 7.4 copy-start.90
  129.5 7.9 copy-start.94
  129.5 9.6 %copy-start.86 = (bf16[1728,1152]{1,0:T(8,128)(2,1)S(1)}, bf16[1728,1152]{1,0:T(8,128)(2,1)}, u32[]{:S(2)}) copy-start(bf16[1728,1152]{1,0:T(8,128)(2,1)} %param.25) | copy-start | bytes 11943940
  145.5 63.1 %all-gather.5.cloned.1.call-start = ((), (), s32[]{:S(2)}) async-start(), calls=%async_computation.13 | async-start | bytes 2949120 | tf_op jit(solution)/shard_map/all_gather | solution.py:159
  184.4 84.1 %reduce-scatter.10.cloned.1.call-start = ((), (), s32[]{:S(2)}) async-start(), calls=%async_computation.14 | async-start | bytes 2949120 | tf_op jit(solution)/shard_map/reduce_scatter | solution.py:167
  208.6 14.9 %copy-start.87 = (bf16[1152,1728]{0,1:T(8,128)(2,1)S(1)}, bf16[1152,1728]{0,1:T(8,128)(2,1)}, u32[]{:S(2)}) copy-start(bf16[1152,1728]{0,1:T(8,128)(2,1)} %param.23) | copy-start | bytes 11943940
  223.5 5.2 copy-start.92
  223.5 5.2 copy-start.95
  223.5 5.2 copy-start.89
  276.0 6.1 copy-start.73
  276.0 6.1 copy-start.75
  276.0 6.2 copy-start.77
  276.0 6.2 copy-start.79
  276.9 15.1 %copy-start.7 = (f32[512,1024]{1,0:T(8,128)S(1)}, f32[512,1024]{1,0:T(8,128)}, u32[]{:S(2)}) copy-start(f32[512,1024]{1,0:T(8,128)} %copy-done.6) | copy-start | bytes 6291460
  276.9 15.1 %copy-start.20 = (bf16[1024,256]{1,0:T(8,128)(2,1)S(1)}, bf16[1024,256]{1,0:T(8,128)(2,1)}, u32[]{:S(2)}) copy-start(bf16[1024,256]{1,0:T(8,128)(2,1)} %copy-done.19) | copy-start | bytes 1572868
  277.8 13.2 %all-to-all-start.2 = ((bf16[256,4,256]{2,0,1:T(8,128)(2,1)}), bf16[256,4,256]{2,0,1:T(8,128)(2,1)}, u32[]{:S(2)}, u32[]{:S(2)}) async-start(bf16[256,4,256]{2,0,1:T(8,128)(2,1)} %bitcast.179), calls=%async_computation.4 | async-start | bytes 1048576 | tf_op jit(solution)/shard_map/all_to_all | solution.py:182
  282.1 69.2 %reduce-scatter.12.cloned.1.call-start = ((), (), s32[]{:S(2)}) async-start(), calls=%async_computation.15 | async-start | bytes 655360 | tf_op jit(solution)/shard_map/reduce_scatter | solution.py:206
  299.0 58.1 %reduce-scatter.14.cloned.1.call-start = ((), (), s32[]{:S(2)}) async-start(), calls=%async_computation.16 | async-start | bytes 655360 | tf_op jit(solution)/shard_map/reduce_scatter | solution.py:209
  302.8 137.7 %reduce-scatter.20.cloned.1.call-start = ((), (), s32[]{:S(2)}) async-start(), calls=%async_computation.19 | async-start | bytes 4644864 | tf_op jit(solution)/shard_map/reduce_scatter | solution.py:253
  312.2 219.4 %reduce-scatter.18.cloned.1.call-start = ((), (), s32[]{:S(2)}) async-start(), calls=%async_computation.18 | async-start | bytes 4644864 | tf_op jit(solution)/shard_map/reduce_scatter | solution.py:250
  322.3 300.4 %reduce-scatter.16.cloned.1.call-start = ((), (), s32[]{:S(2)}) async-start(), calls=%async_computation.17 | async-start | bytes 4644864 | tf_op jit(solution)/shard_map/reduce_scatter | solution.py:247
  332.9 5.5 copy-start.17
  332.9 5.5 copy-start.26
  334.9 14.6 %all-to-all-start.3 = ((bf16[4,2,32768]{2,1,0:T(2,128)(2,1)}), bf16[4,2,32768]{2,1,0:T(2,128)(2,1)S(1)}, u32[]{:S(2)}, u32[]{:S(2)}) async-start(bf16[4,2,32768]{2,1,0:T(2,128)(2,1)} %reshape.405), calls=%async_computation.5 | async-start | bytes 1048576 | tf_op jit(solution)/shard_map/all_to_all | solution.py:202
  338.4 514.9 %all-reduce.4.cloned.1.call-start = ((), (), s32[]{:S(2)}) async-start(), calls=%async_computation.20 | async-start | bytes 23592960 | tf_op jit(solution)/shard_map/psum | solution.py:231
  366.6 42.8 %copy-start.69 = (f32[256]{0:T(256)S(1)}, f32[256]{0:T(256)}, u32[]{:S(2)}) copy-start(f32[256]{0:T(256)} %copy-done.68) | copy-start | bytes 3076
  366.6 42.8 %copy-start.12 = (f32[256,1152]{1,0:T(8,128)S(1)}, f32[256,1152]{1,0:T(8,128)}, u32[]{:S(2)}) copy-start(f32[256,1152]{1,0:T(8,128)} %copy-done.11) | copy-start | bytes 3538948
  853.3 8.1 slice-start
  853.3 5.4 copy-start.36
  853.3 8.1 slice-start.1
  (63 other events, 122.1 us)
Sparse Core Ops, SparseCore 0:
  97.2 24.7 all-gather.2
  145.6 32.8 reduce-scatter.7
  184.5 24.0 all-gather.4
  235.7 32.8 reduce-scatter.9
  299.1 21.6 reduce-scatter.11
  323.2 24.2 reduce-scatter.13
  351.0 89.3 reduce-scatter.19
  444.0 87.5 reduce-scatter.17
  535.2 87.5 reduce-scatter.15
  629.6 223.6 all-reduce.3
where the time goes:
time: 881 us; the launch traced here: 872 us
  waiting for transfers between devices  568 us (64%)
  matrix products  106 us (12%)
  blocking collectives  70.7 us (8%)
  local copies, waits for them, and re-layouts  59.4 us (7%)
  other arithmetic  39 us (4%)
  between operations  16.2 us (2%)
  starting transfers between devices  12.8 us (1%)
    psum x1, waiting for transfers between devices, shards(): lax.psum((query_weight_grad, key_weight_grad, value_weight_grad, out_weig...  228 us
    reduce_scatter x1, waiting for transfers between devices, shards(): lax.psum_scatter(gate_grad.astype(jnp.bfloat16), 'dp', scatter_dimension=...  89.1 us
    reduce_scatter x1, waiting for transfers between devices, shards(): lax.psum_scatter(up_grad.astype(jnp.bfloat16), 'dp', scatter_dimension=0,...  89.1 us
    psum x1, blocking collectives, shards(): lax.psum((query_weight_grad, key_weight_grad, value_weight_grad, out_weig...  42.1 us
    dot_general x11, matrix products, product_tn(): lax.dot_general(left, right, (((0,), (0,)), ((), ())), preferred_element_...  41.5 us
    dot_general x11, matrix products, product_nt(): lax.dot_general(left, right, (((1,), (1,)), ((), ())), preferred_element_...  33.4 us
    reduce_scatter x1, waiting for transfers between devices, shards(): lax.psum_scatter((product_nt(gate_grad_low, gate_weight) + product_nt(up_...  33 us
    reduce_scatter x1, waiting for transfers between devices, shards(): lax.psum_scatter(product(lax.slice_in_dim(hidden_low, 0, tok_rows * lax.a...  32.9 us
  transfers between devices with their start and end apart: 13, of which 10 were waited for; matrix products, arithmetic and copies ran while one was open for 8% of the time, Pallas kernels for 0%

commit v1 on v0

--- a/solution.py
+++ b/solution.py
@@ -139,7 +139,12 @@
     attn_branch, attn_pull = jax.vjp(rms_norm, projected, attn_gain)
     after_attn = x_rows + attn_branch
     pre_normed, pre_pull = jax.vjp(rms_norm, after_attn, pre_ff_gain)
-    rows_all = lax.all_gather(pre_normed.astype(low_type), "head", axis=0, tiled=True)
+    rows_all = jnp.concatenate(
+        lax.all_to_all(
+            jnp.stack([pre_normed.astype(low_type)] * lax.axis_size("head")), "head", 0, 0
+        ),
+        axis=0,
+    )
     gate_act = product(rows_all, gate_weight)
     up_act = product(rows_all, up_weight)
     gelu_gate, gelu_pull = jax.vjp(gelu_tanh, gate_act)

time: 881 us -> 885 us (level)
  blocking collectives: 70.7 us -> 102 us
  waiting for transfers between devices: 568 us -> 544 us
    all_to_all x0 -> x1, blocking collectives: none -> 31.4 us  [shards(): lax.all_to_all(jnp.stack([pre_normed.astype(low_type)] * lax.axis_size('h...]
    all_gather x1 -> x0, waiting for transfers between devices: 24.7 us -> none  [shards(): lax.all_gather(pre_normed.astype(low_type), 'head', axis=0, tiled=True)]
    unnamed x205 -> x207, local copies, waits for them, and re-layouts: 32.8 us -> 32.8 us
  transfers between devices with their start and end apart: 13 -> 12, of which waited for: 10 -> 9; matrix products, arithmetic and copies ran while one was open for 8% -> 8% of each run, Pallas kernels for 0% -> 0%
where the time goes in v1:
time: 885 us; the launch traced here: 876 us
  waiting for transfers between devices  544 us (61%)
  matrix products  103 us (12%)
  blocking collectives  102 us (12%)
  local copies, waits for them, and re-layouts  59.6 us (7%)
  other arithmetic  38.2 us (4%)
  between operations  15.9 us (2%)
  starting transfers between devices  12.6 us (1%)
    psum x1, waiting for transfers between devices, shards(): lax.psum((query_weight_grad, key_weight_grad, value_weight_grad, out_weig...  229 us
    reduce_scatter x1, waiting for transfers between devices, shards(): lax.psum_scatter(gate_grad.astype(jnp.bfloat16), 'dp', scatter_dimension=...  89.1 us
    reduce_scatter x1, waiting for transfers between devices, shards(): lax.psum_scatter(up_grad.astype(jnp.bfloat16), 'dp', scatter_dimension=0,...  89.1 us
    psum x1, blocking collectives, shards(): lax.psum((query_weight_grad, key_weight_grad, value_weight_grad, out_weig...  42.2 us
    dot_general x11, matrix products, product_tn(): lax.dot_general(left, right, (((0,), (0,)), ((), ())), preferred_element_...  41.5 us
    reduce_scatter x1, waiting for transfers between devices, shards(): lax.psum_scatter(product(lax.slice_in_dim(hidden_low, 0, tok_rows * lax.a...  33.6 us
    dot_general x11, matrix products, product_nt(): lax.dot_general(left, right, (((1,), (1,)), ((), ())), preferred_element_...  33.4 us
    reduce_scatter x1, waiting for transfers between devices, shards(): lax.psum_scatter((product_nt(gate_grad_low, gate_weight) + product_nt(up_...  33 us
  transfers between devices with their start and end apart: 12, of which 9 were waited for; matrix products, arithmetic and copies ran while one was open for 8% of the time, Pallas kernels for 0%

profile of v1, /device:TPU:0, one launch (start us, length us, event | category | flops | bytes accessed | tf_op | source)
XLA Modules:
  0.0 876.0 jit_solution(11442087228360037804)
XLA Ops:
  13.7 4.4 copy.65
  18.1 3.6 multiply_reduce_fusion.8
  25.6 4.3 all-to-all-start
  30.5 9.1 %gather_fusion = s32[1024]{0:T(1024)} fusion(s32[1024]{0:T(1024)S(1)} %bitcast.162, s32[1024]{0:T(1024)} %iota_clamp_fusion), kind=kCustom, calls=%fused_computation | custom fusion | bytes 12288 | tf_op jit(solution)/shard_map/jit(_take)/gather | solution.py:106
  43.4 9.0 %all_gather.9 = bf16[1024,256]{0,1:T(8,128)(2,1)} all-gather(bf16[256,256]{0,1:T(8,128)(2,1)S(1)} %pad_maximum_fusion.5), channel_id=1, replica_groups=mesh['dp'=8,'head'=4] {'head'}, dimensions={0}, use_global_device_ids=true | all-gather | bytes 655360 | tf_op jit(solution)/shard_map/all_gather | solution.py:108
  52.5 7.3 all_gather.10
  59.7 2.0 fusion.94
  63.6 1.8 copy.54
  65.4 1.9 fusion.96
  73.3 2.0 reshape.409
  75.2 12.3 %all_to_all.59 = bf16[4,2,32768]{2,1,0:T(2,128)(2,1)S(1)} all-to-all(bf16[4,2,32768]{2,1,0:T(2,128)(2,1)} %reshape.409), channel_id=1, replica_groups=mesh['dp'=8,'head'=4] {'head'}, dimensions={0} | all-to-all | bytes 1048576 | tf_op jit(solution)/shard_map/all_to_all | solution.py:134
  87.5 1.8 reshape.410
  89.3 2.1 copy.66
  96.4 31.4 %all_to_all.60 = bf16[4,256,1152]{2,1,0:T(8,128)(2,1)S(1)} all-to-all(bf16[4,256,1152]{2,1,0:T(8,128)(2,1)S(1)} %stack.2), channel_id=1, replica_groups=mesh['dp'=8,'head'=4] {'head'}, dimensions={0} | all-to-all | bytes 4718592 | tf_op jit(solution)/shard_map/all_to_all | solution.py:143
  127.8 4.9 fusion.98
  132.8 7.9 multiply_convert_fusion.1
  142.4 6.3 convolution_convert_fusion.3
  148.8 33.6 %reduce-scatter.8.cloned.1.call-done = bf16[256,1152]{1,0:T(8,128)(2,1)} async-done(((bf16[1024,1152]{1,0:T(8,128)(2,1)}), bf16[256,1152]{1,0:T(8,128)(2,1)}) %reduce-scatter.8.cloned.1.call-update) | async-done | bytes 589840 | tf_op jit(solution)/shard_map/reduce_scatter | solution.py:152
  183.8 2.4 fusion.43
  186.2 2.2 fusion.39
  188.7 23.9 %all-gather.2.cloned.1.call-done = bf16[1024,1152]{1,0:T(8,128)(2,1)} async-done(((bf16[256,1152]{1,0:T(8,128)(2,1)}), bf16[1024,1152]{1,0:T(8,128)(2,1)}) %all-gather.2.cloned.1.call-update) | async-done | bytes 2359312 | tf_op jit(solution)/shard_map/all_gather | solution.py:164
  212.6 14.8 %multiply_convert_fusion = (bf16[1024,1728]{0,1:T(8,128)(2,1)S(1)}, bf16[1024,1728]{0,1:T(8,128)(2,1)S(1)}) fusion(f32[1024,1728]{0,1:T(8,128)} %copy-done.95, f32[1024,1728]{0,1:T(8,128)} %get-tuple-element.71, bf16[1024,1152]{1,0:T(8,128)(2,1)} %all-gather.2.cloned.1.call-done, bf16[1728,1152]{1,0:T(8,128)(2,1)} %param.25), kind=kOutput, calls=%fused_computation.13 | convolution fusion | flops 4119330816 | bytes 27574272 | tf_op jit(solution)/shard_map/dot_general | solution.py:59
  227.5 5.2 fusion.99
  232.7 6.8 add_convert_fusion
  239.6 33.0 %reduce-scatter.10.cloned.1.call-done = bf16[256,1152]{1,0:T(8,128)(2,1)} async-done(((bf16[1024,1152]{1,0:T(8,128)(2,1)}), bf16[256,1152]{1,0:T(8,128)(2,1)}) %reduce-scatter.10.cloned.1.call-update) | async-done | bytes 589840 | tf_op jit(solution)/shard_map/reduce_scatter | solution.py:172
  272.6 2.5 fusion.34
  275.8 3.9 multiply_reduce_fusion.2
  281.8 4.3 all-to-all-start.3
  286.2 8.8 all-to-all-done.3
  303.1 2.2 fusion.52
  306.8 9.4 %convolution_convert_fusion = bf16[1728,1152]{0,1:T(8,128)(2,1)} fusion(bf16[1024,1728]{0,1:T(8,128)(2,1)} %copy-done.94, bf16[1024,1152]{1,0:T(8,128)(2,1)} %all-gather.2.cloned.1.call-done), kind=kOutput, calls=%fused_computation.3 | convolution fusion | flops 4078854144 | bytes 9879552 | tf_op jit(solution)/shard_map/dot_general | solution.py:53
  317.9 8.4 convolution_convert_fusion.1
  326.4 8.2 convolution_convert_fusion.2
  338.9 3.5 all-to-all-start.4
  342.5 3.0 fusion.102
  345.5 7.9 all-to-all-done.4
  361.1 2.5 fusion.85
  363.6 3.1 fusion.59
  371.3 42.2 %all-reduce = (f32[1152]{0:T(1024)}, f32[256]{0:T(256)}, f32[256]{0:T(256)}, f32[1152]{0:T(1024)}, f32[1152]{0:T(1024)}, /*index=5*/f32[1152]{0:T(1024)}) all-reduce(f32[1152]{0:T(1024)S(1)} %get-tuple-element.21, f32[256]{0:T(256)S(1)} %get-tuple-element.17, ...), channel_id=1, replica_groups=mesh['dp'=8,'head'=4] {'dp','head'}, use_global_device_ids=true, to_apply=%region_32.33 | all-reduce | flops 5120 | bytes 40960 | tf_op jit(solution)/shard_map/psum | solution.py:236
  414.8 29.4 %reduce-scatter.20.cloned.1.call-done = bf16[1728,144]{0,1:T(8,128)(2,1)} async-done(((bf16[1728,1152]{0,1:T(8,128)(2,1)}), bf16[1728,144]{0,1:T(8,128)(2,1)}) %reduce-scatter.20.cloned.1.call-update) | async-done | bytes 497680 | tf_op jit(solution)/shard_map/reduce_scatter | solution.py:258
  444.2 2.1 convert_element_type.202
  446.2 89.1 %reduce-scatter.18.cloned.1.call-done = bf16[144,1728]{1,0:T(8,128)(2,1)} async-done(((bf16[1152,1728]{1,0:T(8,128)(2,1)}), bf16[144,1728]{1,0:T(8,128)(2,1)}) %reduce-scatter.18.cloned.1.call-update) | async-done | bytes 497680 | tf_op jit(solution)/shard_map/reduce_scatter | solution.py:255
  535.3 2.1 convert_element_type.200
  537.4 89.1 %reduce-scatter.16.cloned.1.call-done = bf16[144,1728]{1,0:T(8,128)(2,1)} async-done(((bf16[1152,1728]{1,0:T(8,128)(2,1)}), bf16[144,1728]{1,0:T(8,128)(2,1)}) %reduce-scatter.16.cloned.1.call-update) | async-done | bytes 497680 | tf_op jit(solution)/shard_map/reduce_scatter | solution.py:252
  626.4 2.1 convert_element_type.198
  628.5 229.3 %all-reduce.4.cloned.1.call-done = (f32[1152,1024]{1,0:T(8,128)}, f32[1152,256]{1,0:T(8,128)}, f32[1152,256]{1,0:T(8,128)}, f32[1024,1152]{1,0:T(8,128)}) async-done(((f32[1152,1024]{1,0:T(8,128)}, f32[1152,256]{1,0:T(8,128)}, f32[1152,256]{1,0:T(8,128)}, f32[1024,1152]{1,0:T(8,128)}), (f32[1152,1024]{1,0:T(8,128)}, f32[1152,256]{1,0:T(8,128)}, f32[1152,256]{1,0:T(8,128)}, ...) | async-done | bytes 11796496 | tf_op jit(solution)/shard_map/psum | solution.py:236
  857.8 5.4 copy.76
  865.9 2.4 copy.79
  (307 shorter events, 65.7 us)
Async XLA Ops:
  7.2 85.5 %copy-start = (bf16[1024,1152]{1,0:T(8,128)(2,1)S(1)}, bf16[1024,1152]{1,0:T(8,128)(2,1)}, u32[]{:S(2)}) copy-start(bf16[1024,1152]{1,0:T(8,128)(2,1)} %param.22) | copy-start | bytes 7077892
  7.2 14.8 %copy-start.86 = (f32[128]{0:T(128)}, f32[128]{0:T(128)S(1)}, u32[]{:S(2)}) copy-start(f32[128]{0:T(128)S(1)} %multiply_power_fusion) | copy-start | bytes 1540
  9.8 8.3 copy-start.52
  13.7 4.4 copy-start.82
  13.7 8.2 copy-start.27
  13.7 8.1 copy-start.57
  13.7 4.4 copy-start.3
  13.7 4.4 copy-start.48
  18.1 5.1 copy-start.63
  24.6 5.9 copy-start.2
  25.6 34.1 %all-to-all-start = ((bf16[256,4,256]{0,2,1:T(8,128)(2,1)}), bf16[256,4,256]{0,2,1:T(8,128)(2,1)}, u32[]{:S(2)}, u32[]{:S(2)}) async-start(bf16[256,4,256]{0,2,1:T(8,128)(2,1)} %pad_maximum_fusion.1), calls=%async_computation | async-start | bytes 1048576 | tf_op jit(solution)/shard_map/all_to_all | solution.py:105
  29.9 152.6 %reduce-scatter.8.cloned.1.call-start = ((), (), s32[]{:S(2)}) async-start(), calls=%async_computation.12 | async-start | bytes 2949120 | tf_op jit(solution)/shard_map/reduce_scatter | solution.py:152
  30.5 10.9 %copy-start.42 = (bf16[1152,256]{1,0:T(8,128)(2,1)S(1)}, bf16[1152,256]{1,0:T(8,128)(2,1)}, u32[]{:S(2)}) copy-start(bf16[1152,256]{1,0:T(8,128)(2,1)} %param.21) | copy-start | bytes 1769476
  42.5 22.8 %copy-start.85 = (s32[512]{0:T(512)S(1)}, s32[512]{0:T(512)}, u32[]{:S(2)}) copy-start(s32[512]{0:T(512)} %slice.99) | copy-start | bytes 6148
  59.7 10.6 %copy-start.19 = (bf16[1024,256]{1,0:T(8,128)(2,1)}, bf16[1024,256]{1,0:T(8,128)(2,1)S(1)}, u32[]{:S(2)}) copy-start(bf16[1024,256]{1,0:T(8,128)(2,1)S(1)} %all_gather.10) | copy-start | bytes 1572868
  96.4 31.4 %copy-start.89 = (bf16[1152,1728]{0,1:T(8,128)(2,1)S(1)}, bf16[1152,1728]{0,1:T(8,128)(2,1)}, u32[]{:S(2)}) copy-start(bf16[1152,1728]{0,1:T(8,128)(2,1)} %param.23) | copy-start | bytes 11943940
  127.8 4.9 copy-start.31
  127.8 4.9 copy-start.91
  132.8 7.9 copy-start.95
  132.8 9.6 %copy-start.88 = (bf16[1728,1152]{1,0:T(8,128)(2,1)S(1)}, bf16[1728,1152]{1,0:T(8,128)(2,1)}, u32[]{:S(2)}) copy-start(bf16[1728,1152]{1,0:T(8,128)(2,1)} %param.25) | copy-start | bytes 11943940
  148.8 63.9 %all-gather.2.cloned.1.call-start = ((), (), s32[]{:S(2)}) async-start(), calls=%async_computation.13 | async-start | bytes 2949120 | tf_op jit(solution)/shard_map/all_gather | solution.py:164
  188.4 84.1 %reduce-scatter.10.cloned.1.call-start = ((), (), s32[]{:S(2)}) async-start(), calls=%async_computation.14 | async-start | bytes 2949120 | tf_op jit(solution)/shard_map/reduce_scatter | solution.py:172
  212.6 14.9 %copy-start.90 = (bf16[1152,1728]{0,1:T(8,128)(2,1)S(1)}, bf16[1152,1728]{0,1:T(8,128)(2,1)}, u32[]{:S(2)}) copy-start(bf16[1152,1728]{0,1:T(8,128)(2,1)} %param.23) | copy-start | bytes 11943940
  227.5 5.2 copy-start.93
  227.5 5.2 copy-start.96
  227.5 5.2 copy-start.92
  275.8 3.9 copy-start.51
  280.0 6.1 copy-start.75
  280.0 6.1 copy-start.77
  280.0 6.1 copy-start.79
  280.0 6.1 copy-start.81
  280.9 15.1 %copy-start.7 = (f32[512,1024]{1,0:T(8,128)S(1)}, f32[512,1024]{1,0:T(8,128)}, u32[]{:S(2)}) copy-start(f32[512,1024]{1,0:T(8,128)} %copy-done.6) | copy-start | bytes 6291460
  280.9 15.1 %copy-start.20 = (bf16[1024,256]{1,0:T(8,128)(2,1)S(1)}, bf16[1024,256]{1,0:T(8,128)(2,1)}, u32[]{:S(2)}) copy-start(bf16[1024,256]{1,0:T(8,128)(2,1)} %copy-done.19) | copy-start | bytes 1572868
  281.8 13.2 %all-to-all-start.3 = ((bf16[256,4,256]{2,0,1:T(8,128)(2,1)}), bf16[256,4,256]{2,0,1:T(8,128)(2,1)}, u32[]{:S(2)}, u32[]{:S(2)}) async-start(bf16[256,4,256]{2,0,1:T(8,128)(2,1)} %bitcast.184), calls=%async_computation.5 | async-start | bytes 1048576 | tf_op jit(solution)/shard_map/all_to_all | solution.py:187
  286.1 69.2 %reduce-scatter.12.cloned.1.call-start = ((), (), s32[]{:S(2)}) async-start(), calls=%async_computation.15 | async-start | bytes 655360 | tf_op jit(solution)/shard_map/reduce_scatter | solution.py:211
  303.0 58.1 %reduce-scatter.14.cloned.1.call-start = ((), (), s32[]{:S(2)}) async-start(), calls=%async_computation.16 | async-start | bytes 655360 | tf_op jit(solution)/shard_map/reduce_scatter | solution.py:214
  306.8 137.4 %reduce-scatter.20.cloned.1.call-start = ((), (), s32[]{:S(2)}) async-start(), calls=%async_computation.19 | async-start | bytes 4644864 | tf_op jit(solution)/shard_map/reduce_scatter | solution.py:258
  316.2 219.1 %reduce-scatter.18.cloned.1.call-start = ((), (), s32[]{:S(2)}) async-start(), calls=%async_computation.18 | async-start | bytes 4644864 | tf_op jit(solution)/shard_map/reduce_scatter | solution.py:255
  326.3 300.1 %reduce-scatter.16.cloned.1.call-start = ((), (), s32[]{:S(2)}) async-start(), calls=%async_computation.17 | async-start | bytes 4644864 | tf_op jit(solution)/shard_map/reduce_scatter | solution.py:252
  336.9 5.5 copy-start.17
  336.9 5.5 copy-start.26
  338.9 14.5 %all-to-all-start.4 = ((bf16[4,2,32768]{2,1,0:T(2,128)(2,1)}), bf16[4,2,32768]{2,1,0:T(2,128)(2,1)S(1)}, u32[]{:S(2)}, u32[]{:S(2)}) async-start(bf16[4,2,32768]{2,1,0:T(2,128)(2,1)} %reshape.411), calls=%async_computation.6 | async-start | bytes 1048576 | tf_op jit(solution)/shard_map/all_to_all | solution.py:207
  342.4 515.4 %all-reduce.4.cloned.1.call-start = ((), (), s32[]{:S(2)}) async-start(), calls=%async_computation.20 | async-start | bytes 23592960 | tf_op jit(solution)/shard_map/psum | solution.py:236
  370.6 42.9 %copy-start.71 = (f32[256]{0:T(256)S(1)}, f32[256]{0:T(256)}, u32[]{:S(2)}) copy-start(f32[256]{0:T(256)} %copy-done.70) | copy-start | bytes 3076
  370.6 42.9 %copy-start.12 = (f32[256,1152]{1,0:T(8,128)S(1)}, f32[256,1152]{1,0:T(8,128)}, u32[]{:S(2)}) copy-start(f32[256,1152]{1,0:T(8,128)} %copy-done.11) | copy-start | bytes 3538948
  857.8 8.1 slice-start
  857.8 5.4 copy-start.38
  857.8 8.1 slice-start.1
  (63 other events, 116.4 us)
Sparse Core Ops, SparseCore 0:
  148.9 33.5 reduce-scatter.7
  188.6 24.0 all-gather.1
  239.7 32.8 reduce-scatter.9
  303.1 21.6 reduce-scatter.11
  327.1 24.2 reduce-scatter.13
  354.9 89.2 reduce-scatter.19
  447.7 87.5 reduce-scatter.17
  538.9 87.5 reduce-scatter.15
  633.4 224.3 all-reduce.3
